TPU v7x, 32 devices: a whole 2x2x4 slice. The times are simulated.
32 devices in a mesh: dp: 16 (over z, y, x), mp: 2 (over core).
Axes of the slice: x: 2, y: 2, z: 4, core: 2. Of those that a mesh axis runs over, the one named last changes fastest.
Arguments:
- inputs: bfloat16 [6144, 768], P('dp')
- cotangent: bfloat16 [6144, 768], P('dp'), may hold values from -6 to 6
- lengths: int32 [16, 3], P('dp'), may hold values from 0 to 192, as said below
- masked: int32 [6144], P('dp'), may hold values 0 or 1
- replace_ids: int32 [6144], P('dp'), may hold values from 0 to 15359, as said below
- attention_master: float32 [4, 768, 768], P(None, 'dp', 'mp')
- attention_moment: float32 [4, 768, 768], P(None, 'dp', 'mp'), may hold values from -0.1875 to 0.1875
- attention_square: float32 [4, 768, 768], P(None, 'dp', 'mp'), may hold values from 0.00016276042 to 0.0006510417
- geglu_master: float32 [3, 768, 3072], P(None, 'dp', 'mp')
- geglu_moment: float32 [3, 768, 3072], P(None, 'dp', 'mp'), may hold values from -0.1875 to 0.1875
- geglu_square: float32 [3, 768, 3072], P(None, 'dp', 'mp'), may hold values from 0.00016276042 to 0.0006510417
- embed_master: float32 [15360, 768], P('dp', 'mp'), may hold values from -6 to 6
- embed_moment: float32 [15360, 768], P('dp', 'mp'), may hold values from -0.0008544922 to 0.0008544922
- embed_square: float32 [15360, 768], P('dp', 'mp'), may hold values from 3.1789145e-09 to 1.2715658e-08
- norms_master: float32 [4, 768], replicated
- norms_moment: float32 [4, 768], replicated, may hold values from -0.1875 to 0.1875
- norms_square: float32 [4, 768], replicated, may hold values from 0.00016276042 to 0.0006510417
Outputs:
- output: float32 [6144, 768], P('dp')
- input_grad: float32 [6144, 768], P('dp')
- rms_stats: float32 [3], replicated
- lamb_norms: float32 [2, 12], replicated
- attention_grad: float32 [4, 768, 768], P(None, 'dp', 'mp')
- attention_first: float32 [4, 768, 768], P(None, 'dp', 'mp')
- attention_second: float32 [4, 768, 768], P(None, 'dp', 'mp')
- attention_new: float32 [4, 768, 768], P(None, 'dp', 'mp')
- geglu_grad: float32 [3, 768, 3072], P(None, 'dp', 'mp')
- geglu_first: float32 [3, 768, 3072], P(None, 'dp', 'mp')
- geglu_second: float32 [3, 768, 3072], P(None, 'dp', 'mp')
- geglu_new: float32 [3, 768, 3072], P(None, 'dp', 'mp')
- embed_grad: float32 [15360, 768], P('dp', 'mp')
- embed_first: float32 [15360, 768], P('dp', 'mp')
- embed_second: float32 [15360, 768], P('dp', 'mp')
- embed_new: float32 [15360, 768], P('dp', 'mp')
- norms_grad: float32 [4, 768], replicated
- norms_first: float32 [4, 768], replicated
- norms_second: float32 [4, 768], replicated
- norms_new: float32 [4, 768], replicated
Inputs may be any that keep to these rules, and one draw needn't show every extreme that they name: Row d lists the lengths of the sequences given to device d, zeros after; each sequence has 128 tokens or more; a row sums to at most 384, and some row reaches it with a sequence of 192. `replace_ids`: among the 384 slots of one device, exactly 24 ids fall in each aligned block of 960 table rows.
All inputs are finite; a program needn't handle non-finite values. No bound on the sum of `masked` on one device may be relied on, other than what follows from the above.
Results may differ from a plain program's by a relative error of at most 0.016.
The roundings to bfloat16 on the way count: a program that leaves them out, or rounds other values in their place, can miss the bound.
Values may be sent and summed in bfloat16 or wider, within the bound.
A program may use at most 192 MiB of HBM per device.

v0:
```python
import math
import jax
import jax.numpy as jnp
from jax import lax
from jax.sharding import PartitionSpec as P

HEADS = 12
STEP_COUNT = 6
first_decay = 0.5
second_decay = 0.5
learn_rate = 0.3
matrix_decay = 0.01
adam_epsilon = 1e-06
norm_epsilon = 1e-12
masked_score = -1000000000.0


def cut_along(value, dim, length):
    dims = value.shape
    tiles = value.reshape(*dims[:dim], length, dims[dim] // length, *dims[dim + 1 :])
    return jnp.moveaxis(tiles, dim, 0)


def sent_and_summed(value, axis, dim):
    length = lax.axis_size(axis)
    tiles = lax.all_to_all(cut_along(value, dim, length), axis, 0, 0, tiled=True)
    return jnp.sum(tiles.astype(jnp.float32), axis=0)


def layer_norm(values, gain_row, shift_row):
    center = values - jnp.mean(values, axis=-1, keepdims=True)
    spread = jnp.mean(center * center, axis=-1, keepdims=True)
    return center * lax.rsqrt(spread + norm_epsilon) * gain_row + shift_row


def norm_pair(values, gain_pair):
    return layer_norm(values, gain_pair[0], gain_pair[1])


def lamb_parts(master, moment, square, gradient, decay_rate):
    new_moment = first_decay * moment + (1.0 - first_decay) * gradient
    new_square = second_decay * square + (1.0 - second_decay) * gradient * gradient
    update = (
        new_moment
        / (1.0 - first_decay**STEP_COUNT)
        / (jnp.sqrt(new_square / (1.0 - second_decay**STEP_COUNT)) + adam_epsilon)
        + decay_rate * master
    )
    return (new_moment, new_square, update)


def gelu_tanh(values):
    return jax.nn.gelu(values, approximate=True)


def local(
    inputs,
    cotangent,
    lengths,
    masked,
    replace_ids,
    attention_master,
    attention_moment,
    attention_square,
    geglu_master,
    geglu_moment,
    geglu_square,
    embed_master,
    embed_moment,
    embed_square,
    norms_master,
    norms_moment,
    norms_square,
):
    half_type = jnp.bfloat16
    full_type = jnp.float32
    tokens_here = inputs.shape[0]
    width = inputs.shape[1]
    head_dim = width // HEADS
    local_heads = HEADS // lax.axis_size("mp")
    block_len = min(tokens_here, 512)
    attn_scale = 1.0 / math.sqrt(head_dim)
    column_count = embed_master.shape[1]
    attn_low, geglu_low = (
        lax.all_gather(attention_master.astype(half_type), "dp", axis=1, tiled=True),
        lax.all_gather(geglu_master.astype(half_type), "dp", axis=1, tiled=True),
    )
    table_low = lax.all_gather(embed_master.astype(half_type), "dp", axis=0, tiled=True)
    looked_cols = jnp.take(table_low, replace_ids, axis=0)
    looked = lax.all_gather(looked_cols, "mp", axis=1, tiled=True)
    is_masked = masked[:, None] == 1
    hidden_in = jnp.where(is_masked, looked.astype(full_type), inputs.astype(full_type))
    length_row = lengths[0]
    places = jnp.arange(tokens_here, dtype=jnp.int32)
    ends_at = jnp.cumsum(length_row)
    segment_ids = jnp.sum((ends_at[None, :] <= places[:, None]).astype(jnp.int32), axis=1)
    live_rows = (places < jnp.sum(length_row)).astype(full_type)[:, None]
    token_count = jnp.sum(length_row).astype(full_type)
    head_ids = lax.axis_index("mp") * local_heads + jnp.arange(local_heads, dtype=jnp.int32)
    slopes = 2.0 ** (-8.0 * (head_ids.astype(full_type) + 1.0) / HEADS)
    act_low = hidden_in.astype(half_type)
    qkv_low = jnp.einsum(
        "td,kdc->ktc", act_low, attn_low[:3], preferred_element_type=full_type
    ).astype(half_type)
    head_vals = qkv_low.reshape(3, tokens_here, local_heads, head_dim)

    def block_scores(begin_at, query_blk):
        query_pos = begin_at + jnp.arange(block_len, dtype=jnp.int32)
        scores = (
            jnp.einsum("qhe,khe->hqk", query_blk, head_vals[1], preferred_element_type=full_type)
            * attn_scale
        )
        distance = jnp.abs(query_pos[:, None] - places[None, :]).astype(full_type)
        scores = scores - slopes[:, None, None] * distance[None]
        same_seq = segment_ids[:, None] == segment_ids[None, :]
        return jnp.where(same_seq[None], scores, masked_score)

    def forward_block(begin_at):
        query_blk = head_vals[0]
        scores = block_scores(begin_at, query_blk)
        top_score = jnp.max(scores, axis=-1, keepdims=True)
        raised = jnp.exp(scores - top_score)
        row_total = jnp.sum(raised, axis=-1, keepdims=True)
        weights = (raised / row_total).astype(half_type)
        context_blk = jnp.einsum(
            "hqk,khe->qhe", weights, head_vals[2], preferred_element_type=full_type
        )
        return (context_blk.astype(half_type), (top_score + jnp.log(row_total))[..., 0])

    starts = jnp.arange(tokens_here // block_len, dtype=jnp.int32) * block_len
    context_blocks, lse_blocks = lax.map(forward_block, starts)
    context = context_blocks.reshape(tokens_here, local_heads * head_dim)
    attn_part = jnp.einsum("tc,dc->td", context, attn_low[3], preferred_element_type=full_type)
    attn_out = lax.psum(attn_part, "mp")
    normed_one, first_back = jax.vjp(norm_pair, hidden_in + attn_out, norms_master[0:2])
    normed_low = normed_one.astype(half_type)
    gate_up = jnp.einsum("td,kdf->ktf", normed_low, geglu_low[:2], preferred_element_type=full_type)
    gelu_val, gelu_back = jax.vjp(gelu_tanh, gate_up[0])
    inner_act = (gelu_val * gate_up[1]).astype(half_type)
    geglu_part = jnp.einsum("tf,df->td", inner_act, geglu_low[2], preferred_element_type=full_type)
    geglu_out = lax.psum(geglu_part, "mp")
    result, second_back = jax.vjp(norm_pair, normed_one + geglu_out, norms_master[2:4])
    squares = jnp.stack(
        [
            jnp.sum(hidden_in * hidden_in * live_rows),
            jnp.sum(attn_out * attn_out * live_rows),
            jnp.sum(geglu_out * geglu_out * live_rows),
        ]
    )
    count_total, square_total = lax.psum((token_count, squares), "dp")
    rms_stats = jnp.sqrt(square_total / (count_total * width) + 1e-06)
    grad_second, norm_grad_two = second_back(cotangent.astype(full_type) * live_rows)
    grad_geglu = grad_second.astype(half_type)
    grad_inner = jnp.einsum("td,df->tf", grad_geglu, geglu_low[2], preferred_element_type=full_type)
    down_grad = jnp.einsum("td,tf->df", grad_geglu, inner_act, preferred_element_type=full_type)
    grad_gate = gelu_back(grad_inner * gate_up[1])[0]
    grad_up = grad_inner * gelu_val
    grad_gu = jnp.stack([grad_gate, grad_up]).astype(half_type)
    gu_grad = jnp.einsum("td,ktf->kdf", normed_low, grad_gu, preferred_element_type=full_type)
    geglu_local = jnp.concatenate([gu_grad, down_grad[None]], axis=0)
    back_part = jnp.einsum("ktf,kdf->td", grad_gu, geglu_low[:2], preferred_element_type=full_type)
    grad_normed = grad_second + lax.psum(back_part, "mp")
    grad_first_in, norm_grad_one = first_back(grad_normed)
    grad_attn = grad_first_in.astype(half_type)
    grad_context = jnp.einsum(
        "td,dc->tc", grad_attn, attn_low[3], preferred_element_type=full_type
    ).astype(half_type)
    out_grad = jnp.einsum("td,tc->dc", grad_attn, context, preferred_element_type=full_type)
    grad_heads = grad_context.reshape(tokens_here, local_heads, head_dim)

    def backward_block(carry, packed):
        key_acc, value_acc = carry
        begin_at, lse_blk = packed
        query_blk = head_vals[0]
        scores = block_scores(begin_at, query_blk)
        weights = jnp.exp(scores - lse_blk[..., None])
        grad_weights = jnp.einsum(
            "qhe,khe->hqk", grad_heads, head_vals[2], preferred_element_type=full_type
        )
        value_acc = value_acc + jnp.einsum(
            "hqk,qhe->khe", weights.astype(half_type), grad_heads, preferred_element_type=full_type
        )
        row_inner = jnp.sum(grad_weights * weights, axis=-1, keepdims=True)
        grad_scores = (weights * (grad_weights - row_inner)).astype(half_type)
        grad_query = (
            jnp.einsum("hqk,khe->qhe", grad_scores, head_vals[1], preferred_element_type=full_type)
            * attn_scale
        )
        key_acc = (
            key_acc
            + jnp.einsum("hqk,qhe->khe", grad_scores, query_blk, preferred_element_type=full_type)
            * attn_scale
        )
        return ((key_acc, value_acc), grad_query.astype(half_type))

    zero_heads = jnp.zeros((tokens_here, local_heads, head_dim), full_type)
    (key_acc, value_acc), query_grads = lax.scan(
        backward_block, (zero_heads, zero_heads), (starts, lse_blocks)
    )
    grad_qkv = jnp.stack(
        [
            query_grads.reshape(tokens_here, -1),
            key_acc.reshape(tokens_here, -1).astype(half_type),
            value_acc.reshape(tokens_here, -1).astype(half_type),
        ]
    )
    qkv_grad = jnp.einsum("td,ktc->kdc", act_low, grad_qkv, preferred_element_type=full_type)
    act_part = jnp.einsum("ktc,kdc->td", grad_qkv, attn_low[:3], preferred_element_type=full_type)
    grad_in = grad_first_in + lax.psum(act_part.astype(jnp.bfloat16), "mp").astype(jnp.float32)
    input_grad = jnp.where(is_masked, 0.0, grad_in)
    attention_local = jnp.concatenate([qkv_grad, out_grad[None]], axis=0)
    own_columns = lax.dynamic_slice_in_dim(
        grad_in, lax.axis_index("mp") * column_count, column_count, 1
    )
    picked = jnp.where(is_masked, own_columns, 0.0)
    embed_local = jax.ops.segment_sum(picked, replace_ids, num_segments=table_low.shape[0])
    embed_summed = lax.psum_scatter(embed_local, "dp", scatter_dimension=0, tiled=True)
    attention_summed, geglu_summed = (
        sent_and_summed(attention_local.astype(jnp.bfloat16), "dp", 1),
        sent_and_summed(geglu_local.astype(jnp.bfloat16), "dp", 1),
    )
    inverse_count = 1.0 / count_total
    attention_grad = attention_summed * inverse_count
    geglu_grad = geglu_summed * inverse_count
    embed_grad = embed_summed * inverse_count
    attention_first, attention_second, attention_update = lamb_parts(
        attention_master, attention_moment, attention_square, attention_grad, matrix_decay
    )
    geglu_first, geglu_second, geglu_update = lamb_parts(
        geglu_master, geglu_moment, geglu_square, geglu_grad, matrix_decay
    )
    embed_first, embed_second, embed_update = lamb_parts(
        embed_master, embed_moment, embed_square, embed_grad, matrix_decay
    )
    weight_squares = jnp.concatenate(
        [
            jnp.sum(attention_master * attention_master, axis=(1, 2)),
            jnp.sum(geglu_master * geglu_master, axis=(1, 2)),
            jnp.sum(embed_master * embed_master)[None],
        ]
    )
    update_squares = jnp.concatenate(
        [
            jnp.sum(attention_update * attention_update, axis=(1, 2)),
            jnp.sum(geglu_update * geglu_update, axis=(1, 2)),
            jnp.sum(embed_update * embed_update)[None],
        ]
    )
    norms_local = jnp.concatenate([norm_grad_one, norm_grad_two], axis=0)
    weight_total, update_total, norms_summed = lax.psum(
        (weight_squares, update_squares, norms_local * 0.5), ("dp", "mp")
    )
    weight_norms = jnp.sqrt(weight_total)
    update_norms = jnp.sqrt(update_total)
    ratios = weight_norms / update_norms
    attention_new = attention_master - learn_rate * ratios[0:4][:, None, None] * attention_update
    geglu_new = geglu_master - learn_rate * ratios[4:7][:, None, None] * geglu_update
    embed_new = embed_master - learn_rate * ratios[7] * embed_update
    norms_grad = norms_summed * inverse_count
    norms_first, norms_second, norms_update = lamb_parts(
        norms_master, norms_moment, norms_square, norms_grad, 0.0
    )
    norm_weight = jnp.sqrt(jnp.sum(norms_master * norms_master, axis=1))
    norm_update = jnp.sqrt(jnp.sum(norms_update * norms_update, axis=1))
    norms_new = norms_master - learn_rate * (norm_weight / norm_update)[:, None] * norms_update
    lamb_norms = jnp.stack(
        [jnp.concatenate([weight_norms, norm_weight]), jnp.concatenate([update_norms, norm_update])]
    )
    return (
        result,
        input_grad,
        rms_stats,
        lamb_norms,
        attention_grad,
        attention_first,
        attention_second,
        attention_new,
        geglu_grad,
        geglu_first,
        geglu_second,
        geglu_new,
        embed_grad,
        embed_first,
        embed_second,
        embed_new,
        norms_grad,
        norms_first,
        norms_second,
        norms_new,
    )


def solution(mesh):
    in_specs = (
        P("dp", None),
        P("dp", None),
        P("dp", None),
        P("dp"),
        P("dp"),
        P(None, "dp", "mp"),
        P(None, "dp", "mp"),
        P(None, "dp", "mp"),
        P(None, "dp", "mp"),
        P(None, "dp", "mp"),
        P(None, "dp", "mp"),
        P("dp", "mp"),
        P("dp", "mp"),
        P("dp", "mp"),
        P(),
        P(),
        P(),
    )
    out_specs = (
        P("dp", None),
        P("dp", None),
        P(),
        P(),
        P(None, "dp", "mp"),
        P(None, "dp", "mp"),
        P(None, "dp", "mp"),
        P(None, "dp", "mp"),
        P(None, "dp", "mp"),
        P(None, "dp", "mp"),
        P(None, "dp", "mp"),
        P(None, "dp", "mp"),
        P("dp", "mp"),
        P("dp", "mp"),
        P("dp", "mp"),
        P("dp", "mp"),
        P(),
        P(),
        P(),
        P(),
    )
    return jax.shard_map(local, mesh=mesh, in_specs=in_specs, out_specs=out_specs, check_vma=False)
```

profile of v0, /device:TPU:0, one launch (start us, length us, event | category | flops | bytes accessed | tf_op | source)
XLA Modules:
  0.0 1076.4 jit_solution(6731088985889812064)
XLA Ops:
  13.5 62.9 %all-gather.6.cloned.1.call-done = bf16[4,768,384]{2,0,1:T(4,128)(2,1)} async-done(((bf16[4,48,384]{2,0,1:T(4,128)(2,1)}), bf16[4,768,384]{2,0,1:T(4,128)(2,1)}) %all-gather.6.cloned.1.call-update) | async-done | bytes 2359312 | tf_op jit(solution)/shard_map/all_gather | solution.py:85
  76.4 5.5 copy.136
  84.1 139.1 %all-gather.4.cloned.1.call-done = bf16[15360,384]{1,0:T(8,128)(2,1)} async-done(((bf16[960,384]{1,0:T(8,128)(2,1)}), bf16[15360,384]{1,0:T(8,128)(2,1)}) %all-gather.4.cloned.1.call-update) | async-done | bytes 11796496 | tf_op jit(solution)/shard_map/all_gather | solution.py:88
  223.2 7.9 gather_fusion
  244.2 14.9 %all-reduce.11.cloned.1.call-done = f32[384,768]{1,0:T(8,128)} async-done(((f32[384,768]{1,0:T(8,128)}), f32[384,768]{1,0:T(8,128)}) %all-reduce.11.cloned.1.call-update) | async-done | bytes 1179664 | tf_op jit(solution)/shard_map/psum | solution.py:134
  262.4 102.8 %all-gather.8.cloned.1.call-done = bf16[3,768,1536]{2,1,0:T(8,128)(2,1)} async-done(((bf16[3,48,1536]{2,1,0:T(8,128)(2,1)}), bf16[3,768,1536]{2,1,0:T(8,128)(2,1)}) %all-gather.8.cloned.1.call-update) | async-done | bytes 7077904 | tf_op jit(solution)/shard_map/all_gather | solution.py:86
  365.1 4.8 fusion.6
  373.1 3.8 fusion.33
  378.9 16.2 %all-reduce.13.cloned.1.call-done = f32[384,768]{1,0:T(8,128)} async-done(((f32[384,768]{1,0:T(8,128)}), f32[384,768]{1,0:T(8,128)}) %all-reduce.13.cloned.1.call-update) | async-done | bytes 1179664 | tf_op jit(solution)/shard_map/psum | solution.py:141
  402.2 4.5 fusion.56
  412.3 20.2 %all-reduce.15.cloned.1.call-done = f32[384,768]{1,0:T(8,128)} async-done(((f32[384,768]{1,0:T(8,128)}), f32[384,768]{1,0:T(8,128)}) %all-reduce.15.cloned.1.call-update) | async-done | bytes 1179664 | tf_op jit(solution)/shard_map/psum | solution.py:162
  432.5 4.1 multiply_reduce_fusion.4
  448.2 20.1 %all-reduce.17.cloned.1.call-done = bf16[384,768]{1,0:T(8,128)(2,1)} async-done(((bf16[384,768]{1,0:T(8,128)(2,1)}), bf16[384,768]{1,0:T(8,128)(2,1)}) %all-reduce.17.cloned.1.call-update) | async-done | bytes 589840 | tf_op jit(solution)/shard_map/psum | solution.py:209
  470.7 12.5 %scatter_custom_fusion = f32[15360,384]{1,0:T(8,128)} fusion(s32[384]{0:T(512)} %param.21, f32[]{:T(128)} %constant.67.clone.1, f32[384,768]{1,0:T(8,128)S(1)} %get-tuple-element.110, s32[]{:T(128)} %constant.48.clone.1, s32[]{:T(128)S(6)} %select_n.36, pred[384]{0:T(512)(128)(4,1)S(1)} %copy-done.69), kind=kCustom, calls=%fused_computation.3 | custom fusion | flops 294912 | bytes 24184836 | tf_op jit(solution)/shard_map/scatter-add | solution.py:216
  492.9 6.9 all-to-all-start
  499.9 6.5 convolution_convert_fusion
  510.4 5.8 maximum_bitcast_fusion
  516.2 66.4 %all-to-all-done = bf16[16,4,48,384]{3,2,1,0:T(8,128)(2,1)S(1)} async-done(((bf16[16,4,48,384]{3,2,1,0:T(8,128)(2,1)}), bf16[16,4,48,384]{3,2,1,0:T(8,128)(2,1)S(1)}, u32[]{:S(2)}, u32[]{:S(2)}) %all-to-all-start) | async-done | bytes 2359328 | tf_op jit(solution)/shard_map/all_to_all | solution.py:26
  582.6 29.9 %all-to-all-start.1 = ((bf16[16,3,48,1536]{3,2,1,0:T(8,128)(2,1)}), bf16[16,3,48,1536]{3,2,1,0:T(8,128)(2,1)}, u32[]{:S(2)}, u32[]{:S(2)}) async-start(bf16[16,3,48,1536]{3,2,1,0:T(8,128)(2,1)} %maximum_bitcast_fusion), calls=%async_computation.1 | async-start | bytes 14155776 | tf_op jit(solution)/shard_map/all_to_all | solution.py:26
  615.2 219.2 %all-reduce.5 = (f32[3]{0:T(128)S(1)}, f32[]{:T(128)}) all-reduce(f32[3]{0:T(128)S(1)} %pad_maximum_fusion.9, f32[]{:T(128)S(6)} %convert_element_type.185), channel_id=1, replica_groups=mesh['dp'=16,'mp'=2] {'dp'}, use_global_device_ids=true, to_apply=%region_21.22 | all-reduce | flops 4 | bytes 32 | tf_op jit(solution)/shard_map/psum | solution.py:150
  839.0 4.8 convert_reduce_fusion
  846.2 164.9 %reduce-scatter.2.cloned.1.call-done = f32[960,384]{1,0:T(8,128)} async-done(((f32[15360,384]{1,0:T(8,128)}), f32[960,384]{1,0:T(8,128)}) %reduce-scatter.2.cloned.1.call-update) | async-done | bytes 1474576 | tf_op jit(solution)/shard_map/reduce_scatter | solution.py:217
  1011.2 5.4 multiply_reduce_fusion.2
  1018.5 39.8 %all-reduce.4 = (f32[4,768]{1,0:T(4,128)}, f32[8]{0:T(128)}, f32[8]{0:T(128)}) all-reduce(f32[4,768]{1,0:T(4,128)} %maximum_multiply_fusion, f32[8]{0:T(128)} %get-tuple-element.142, f32[8]{0:T(128)S(1)} %get-tuple-element.141), channel_id=1, replica_groups=mesh['dp'=16,'mp'=2] {'dp','mp'}, use_global_device_ids=true, to_apply=%region_40.41 | all-reduce | flops 3088 | bytes 24704 | tf_op jit(solution)/shard_map/psum | solution.py:250
  (275 shorter events, 89.4 us)
Async XLA Ops:
  7.2 69.2 %all-gather.6.cloned.1.call-start = ((), (), s32[]{:S(2)}) async-start(), calls=%async_computation.4 | async-start | bytes 2506752 | tf_op jit(solution)/shard_map/all_gather | solution.py:85
  9.0 214.2 %all-gather.4.cloned.1.call-start = ((), (), s32[]{:S(2)}) async-start(), calls=%async_computation.3 | async-start | bytes 12533760 | tf_op jit(solution)/shard_map/all_gather | solution.py:88
  11.4 247.6 %all-reduce.11.cloned.1.call-start = ((), (), s32[]{:S(2)}) async-start(), calls=%async_computation.5 | async-start | bytes 2359296 | tf_op jit(solution)/shard_map/psum | solution.py:134
  12.7 220.8 %copy-start.67 = (pred[384]{0:T(512)(128)(4,1)}, pred[384]{0:T(512)(128)(4,1)S(1)}, u32[]{:S(2)}) copy-start(pred[384]{0:T(512)(128)(4,1)S(1)} %broadcast_compare_fusion.1) | copy-start | bytes 1156
  84.1 149.4 %copy-start.23 = (bf16[384,768]{1,0:T(8,128)(2,1)S(1)}, bf16[384,768]{1,0:T(8,128)(2,1)}, u32[]{:S(2)}) copy-start(bf16[384,768]{1,0:T(8,128)(2,1)} %param.17) | copy-start | bytes 1769476
  84.1 149.4 %copy-start.26 = (bf16[3,768,384]{1,2,0:T(8,128)(2,1)S(1)}, bf16[3,768,384]{1,2,0:T(8,128)(2,1)}, u32[]{:S(2)}) copy-start(bf16[3,768,384]{1,2,0:T(8,128)(2,1)} %copy.136) | copy-start | bytes 5308420
  240.9 124.2 %all-gather.8.cloned.1.call-start = ((), (), s32[]{:S(2)}) async-start(), calls=%async_computation.6 | async-start | bytes 7520256 | tf_op jit(solution)/shard_map/all_gather | solution.py:86
  243.0 152.1 %all-reduce.13.cloned.1.call-start = ((), (), s32[]{:S(2)}) async-start(), calls=%async_computation.7 | async-start | bytes 2359296 | tf_op jit(solution)/shard_map/psum | solution.py:141
  261.1 134.0 %copy-start.47 = (f32[384]{0:T(512)}, f32[384]{0:T(512)S(1)}, u32[]{:S(2)}) copy-start(f32[384]{0:T(512)S(1)} %broadcast_multiply_fusion.5) | copy-start | bytes 4612
  377.0 55.5 %all-reduce.15.cloned.1.call-start = ((), (), s32[]{:S(2)}) async-start(), calls=%async_computation.8 | async-start | bytes 2359296 | tf_op jit(solution)/shard_map/psum | solution.py:162
  411.4 57.0 %all-reduce.17.cloned.1.call-start = ((), (), s32[]{:S(2)}) async-start(), calls=%async_computation.9 | async-start | bytes 1179648 | tf_op jit(solution)/shard_map/psum | solution.py:209
  448.2 563.0 %reduce-scatter.2.cloned.1.call-start = ((), (), s32[]{:S(2)}) async-start(), calls=%async_computation.10 | async-start | bytes 25067520 | tf_op jit(solution)/shard_map/reduce_scatter | solution.py:217
  492.9 89.7 %all-to-all-start = ((bf16[16,4,48,384]{3,2,1,0:T(8,128)(2,1)}), bf16[16,4,48,384]{3,2,1,0:T(8,128)(2,1)S(1)}, u32[]{:S(2)}, u32[]{:S(2)}) async-start(bf16[16,4,48,384]{3,2,1,0:T(8,128)(2,1)} %copy.121), calls=%async_computation | async-start | bytes 4718592 | tf_op jit(solution)/shard_map/all_to_all | solution.py:26
  516.2 318.2 %copy-start.66 = (f32[768]{0:T(1024)S(1)}, f32[768]{0:T(1024)}, u32[]{:S(2)}) copy-start(f32[768]{0:T(1024)} %get-tuple-element.73) | copy-start | bytes 9220
  516.2 319.5 %copy-start.65 = (f32[768]{0:T(1024)S(1)}, f32[768]{0:T(1024)}, u32[]{:S(2)}) copy-start(f32[768]{0:T(1024)} %get-tuple-element.80) | copy-start | bytes 9220
  516.2 320.1 %copy-start.63 = (f32[768]{0:T(1024)S(1)}, f32[768]{0:T(1024)}, u32[]{:S(2)}) copy-start(f32[768]{0:T(1024)} %get-tuple-element.71) | copy-start | bytes 9220
  516.2 320.1 %copy-start.62 = (f32[768]{0:T(1024)S(1)}, f32[768]{0:T(1024)}, u32[]{:S(2)}) copy-start(f32[768]{0:T(1024)} %get-tuple-element.77) | copy-start | bytes 9220
  582.6 256.3 %all-to-all-start.1 = ((bf16[16,3,48,1536]{3,2,1,0:T(8,128)(2,1)}), bf16[16,3,48,1536]{3,2,1,0:T(8,128)(2,1)}, u32[]{:S(2)}, u32[]{:S(2)}) async-start(bf16[16,3,48,1536]{3,2,1,0:T(8,128)(2,1)} %maximum_bitcast_fusion), calls=%async_computation.1 | async-start | bytes 14155776 | tf_op jit(solution)/shard_map/all_to_all | solution.py:26
  612.6 224.7 %copy-start.21 = (f32[4,48,384]{2,1,0:T(8,128)S(1)}, f32[4,48,384]{2,1,0:T(8,128)}, u32[]{:S(2)}) copy-start(f32[4,48,384]{2,1,0:T(8,128)} %param.22) | copy-start | bytes 884740
  612.6 224.7 %copy-start.42 = (f32[4,48,384]{2,1,0:T(8,128)S(1)}, f32[4,48,384]{2,1,0:T(8,128)}, u32[]{:S(2)}) copy-start(f32[4,48,384]{2,1,0:T(8,128)} %param.23) | copy-start | bytes 884740
  612.6 224.7 %copy-start.43 = (f32[4,48,384]{2,1,0:T(8,128)S(1)}, f32[4,48,384]{2,1,0:T(8,128)}, u32[]{:S(2)}) copy-start(f32[4,48,384]{2,1,0:T(8,128)} %param.24) | copy-start | bytes 884740
  843.8 167.4 %copy-start.3 = (f32[960,384]{1,0:T(8,128)S(1)}, f32[960,384]{1,0:T(8,128)}, u32[]{:S(2)}) copy-start(f32[960,384]{1,0:T(8,128)} %param.28) | copy-start | bytes 4423684
  846.2 219.0 %copy-start.19 = (f32[3,48,1536]{2,1,0:T(8,128)}, f32[3,48,1536]{2,1,0:T(8,128)S(1)}, u32[]{:S(2)}) copy-start(f32[3,48,1536]{2,1,0:T(8,128)S(1)} %get-tuple-element.103) | copy-start | bytes 2654212
  846.2 214.1 %copy-start.46 = (f32[4,768]{1,0:T(4,128)S(1)}, f32[4,768]{1,0:T(4,128)}, u32[]{:S(2)}) copy-start(f32[4,768]{1,0:T(4,128)} %param.31) | copy-start | bytes 36868
  (71 other events, 527.5 us)
Sparse Core Ops, SparseCore 0:
  11.4 64.9 all-gather.5
  79.8 143.3 all-gather.3
  241.1 17.9 all-reduce.10
  262.6 102.5 all-gather.7
  377.1 17.9 all-reduce.12
  411.5 20.9 all-reduce.14
  448.3 20.0 all-reduce.16
  483.5 527.6 reduce-scatter.1
where the time goes:
time: 1080 us
  waiting for transfers between devices  608 us (56%)
  blocking collectives  261 us (24%)
  other arithmetic  73.6 us (7%)
  matrix products  39.9 us (4%)
  local copies, waits for them, and re-layouts  38.1 us (4%)
  starting transfers between devices  37.9 us (4%)
  between operations  18.1 us (2%)
    psum x1, blocking collectives, local(): count_total, square_total = lax.psum((token_count, squares), 'dp')  219 us
    reduce_scatter x1, waiting for transfers between devices, local(): lax.psum_scatter(embed_local, 'dp', scatter_dimension=0, tiled=True)  165 us
    all_gather x1, waiting for transfers between devices, local(): lax.all_gather(embed_master.astype(half_type), 'dp', axis=0, tiled=True)  139 us
    all_gather x1, waiting for transfers between devices, local(): lax.all_gather(geglu_master.astype(half_type), 'dp', axis=1, tiled=True)  103 us
    all_to_all x2, waiting for transfers between devices, sent_and_summed(): lax.all_to_all(cut_along(value, dim, length), axis, 0, 0, tiled=True)  66.4 us
    all_gather x1, waiting for transfers between devices, local(): lax.all_gather(attention_master.astype(half_type), 'dp', axis=1, tiled=True)  62.9 us
    psum x1, blocking collectives, local(): lax.psum((weight_squares, update_squares, norms_local * 0.5), ('dp', 'mp'))  39.8 us
    all_to_all x2, starting transfers between devices, sent_and_summed(): lax.all_to_all(cut_along(value, dim, length), axis, 0, 0, tiled=True)  36.9 us
  transfers between devices with their start and end apart: 10, of which 9 were waited for; matrix products, arithmetic and copies ran while one was open for 5% of the time, Pallas kernels for 0%

commit v1 on v0

--- a/solution.py
+++ b/solution.py
@@ -248,7 +248,7 @@
     )
     norms_local = jnp.concatenate([norm_grad_one, norm_grad_two], axis=0)
     weight_total, update_total, norms_summed = lax.psum(
-        (weight_squares, update_squares, norms_local * 0.5), ("dp", "mp")
+        lax.psum((weight_squares, update_squares, norms_local * 0.5), "mp"), "dp"
     )
     weight_norms = jnp.sqrt(weight_total)
     update_norms = jnp.sqrt(update_total)

time: 1080 us -> 1130 us (1.046)
  blocking collectives: 261 us -> 303 us
    psum x1 -> x2, blocking collectives: 219 us -> 296 us  [local(): count_total, square_total = lax.psum((token_count, squares), 'dp')]
    psum x1, blocking collectives: 39.8 us -> 4.57 us  [local(): lax.psum((weight_squares, update_squares, norms_local * 0.5), 'mp')]
where the time goes in v1:
time: 1130 us; the launch traced here: 1120 us
  waiting for transfers between devices  606 us (54%)
  blocking collectives  303 us (27%)
  other arithmetic  74.3 us (7%)
  matrix products  39.9 us (4%)
  local copies, waits for them, and re-layouts  38.1 us (3%)
  starting transfers between devices  37.9 us (3%)
  between operations  18.2 us (2%)
    psum x2, blocking collectives, local(): count_total, square_total = lax.psum((token_count, squares), 'dp')  296 us
    reduce_scatter x1, waiting for transfers between devices, local(): lax.psum_scatter(embed_local, 'dp', scatter_dimension=0, tiled=True)  163 us
    all_gather x1, waiting for transfers between devices, local(): lax.all_gather(embed_master.astype(half_type), 'dp', axis=0, tiled=True)  139 us
    all_gather x1, waiting for transfers between devices, local(): lax.all_gather(geglu_master.astype(half_type), 'dp', axis=1, tiled=True)  103 us
    all_to_all x2, waiting for transfers between devices, sent_and_summed(): lax.all_to_all(cut_along(value, dim, length), axis, 0, 0, tiled=True)  66.4 us
    all_gather x1, waiting for transfers between devices, local(): lax.all_gather(attention_master.astype(half_type), 'dp', axis=1, tiled=True)  62.9 us
    all_to_all x2, starting transfers between devices, sent_and_summed(): lax.all_to_all(cut_along(value, dim, length), axis, 0, 0, tiled=True)  36.9 us
  transfers between devices with their start and end apart: 10, of which 9 were waited for; matrix products, arithmetic and copies ran while one was open for 5% of the time, Pallas kernels for 0%

profile of v1, /device:TPU:0, one launch (start us, length us, event | category | flops | bytes accessed | tf_op | source)
XLA Modules:
  0.0 1117.3 jit_solution(4738766813360312366)
XLA Ops:
  13.5 62.9 %all-gather.6.cloned.1.call-done = bf16[4,768,384]{2,0,1:T(4,128)(2,1)} async-done(((bf16[4,48,384]{2,0,1:T(4,128)(2,1)}), bf16[4,768,384]{2,0,1:T(4,128)(2,1)}) %all-gather.6.cloned.1.call-update) | async-done | bytes 2359312 | tf_op jit(solution)/shard_map/all_gather | solution.py:85
  76.4 5.4 copy.136
  84.1 139.1 %all-gather.4.cloned.1.call-done = bf16[15360,384]{1,0:T(8,128)(2,1)} async-done(((bf16[960,384]{1,0:T(8,128)(2,1)}), bf16[15360,384]{1,0:T(8,128)(2,1)}) %all-gather.4.cloned.1.call-update) | async-done | bytes 11796496 | tf_op jit(solution)/shard_map/all_gather | solution.py:88
  223.2 7.9 gather_fusion
  244.2 14.9 %all-reduce.11.cloned.1.call-done = f32[384,768]{1,0:T(8,128)} async-done(((f32[384,768]{1,0:T(8,128)}), f32[384,768]{1,0:T(8,128)}) %all-reduce.11.cloned.1.call-update) | async-done | bytes 1179664 | tf_op jit(solution)/shard_map/psum | solution.py:134
  262.4 102.8 %all-gather.8.cloned.1.call-done = bf16[3,768,1536]{2,1,0:T(8,128)(2,1)} async-done(((bf16[3,48,1536]{2,1,0:T(8,128)(2,1)}), bf16[3,768,1536]{2,1,0:T(8,128)(2,1)}) %all-gather.8.cloned.1.call-update) | async-done | bytes 7077904 | tf_op jit(solution)/shard_map/all_gather | solution.py:86
  365.1 4.8 fusion.6
  378.9 16.2 %all-reduce.13.cloned.1.call-done = f32[384,768]{1,0:T(8,128)} async-done(((f32[384,768]{1,0:T(8,128)}), f32[384,768]{1,0:T(8,128)}) %all-reduce.13.cloned.1.call-update) | async-done | bytes 1179664 | tf_op jit(solution)/shard_map/psum | solution.py:141
  402.3 4.5 fusion.56
  412.3 20.2 %all-reduce.15.cloned.1.call-done = f32[384,768]{1,0:T(8,128)} async-done(((f32[384,768]{1,0:T(8,128)}), f32[384,768]{1,0:T(8,128)}) %all-reduce.15.cloned.1.call-update) | async-done | bytes 1179664 | tf_op jit(solution)/shard_map/psum | solution.py:162
  432.5 4.1 multiply_reduce_fusion.4
  448.3 20.1 %all-reduce.17.cloned.1.call-done = bf16[384,768]{1,0:T(8,128)(2,1)} async-done(((bf16[384,768]{1,0:T(8,128)(2,1)}), bf16[384,768]{1,0:T(8,128)(2,1)}) %all-reduce.17.cloned.1.call-update) | async-done | bytes 589840 | tf_op jit(solution)/shard_map/psum | solution.py:209
  470.8 12.5 %scatter_custom_fusion = f32[15360,384]{1,0:T(8,128)} fusion(s32[384]{0:T(512)} %param.21, f32[]{:T(128)} %constant.67.clone.1, f32[384,768]{1,0:T(8,128)S(1)} %get-tuple-element.112, s32[]{:T(128)} %constant.48.clone.1, s32[]{:T(128)S(6)} %select_n.36, pred[384]{0:T(512)(128)(4,1)S(1)} %copy-done.69), kind=kCustom, calls=%fused_computation.3 | custom fusion | flops 294912 | bytes 24184836 | tf_op jit(solution)/shard_map/scatter-add | solution.py:216
  492.9 6.9 all-to-all-start
  499.8 6.5 convolution_convert_fusion
  510.4 5.8 maximum_bitcast_fusion
  516.2 66.4 %all-to-all-done = bf16[16,4,48,384]{3,2,1,0:T(8,128)(2,1)S(1)} async-done(((bf16[16,4,48,384]{3,2,1,0:T(8,128)(2,1)}), bf16[16,4,48,384]{3,2,1,0:T(8,128)(2,1)S(1)}, u32[]{:S(2)}, u32[]{:S(2)}) %all-to-all-start) | async-done | bytes 2359328 | tf_op jit(solution)/shard_map/all_to_all | solution.py:26
  582.6 29.9 %all-to-all-start.1 = ((bf16[16,3,48,1536]{3,2,1,0:T(8,128)(2,1)}), bf16[16,3,48,1536]{3,2,1,0:T(8,128)(2,1)}, u32[]{:S(2)}, u32[]{:S(2)}) async-start(bf16[16,3,48,1536]{3,2,1,0:T(8,128)(2,1)} %maximum_bitcast_fusion), calls=%async_computation.1 | async-start | bytes 14155776 | tf_op jit(solution)/shard_map/all_to_all | solution.py:26
  613.3 221.6 %psum.89 = f32[]{:T(128)} all-reduce(f32[]{:T(128)S(6)} %convert_element_type.185), channel_id=1, replica_groups=mesh['dp'=16,'mp'=2] {'dp'}, use_global_device_ids=true, to_apply=%region_22.23 | all-reduce | flops 1 | bytes 8 | tf_op jit(solution)/shard_map/psum | solution.py:150
  841.0 4.7 convert_reduce_fusion
  848.2 163.1 %reduce-scatter.2.cloned.1.call-done = f32[960,384]{1,0:T(8,128)} async-done(((f32[15360,384]{1,0:T(8,128)}), f32[960,384]{1,0:T(8,128)}) %reduce-scatter.2.cloned.1.call-update) | async-done | bytes 1474576 | tf_op jit(solution)/shard_map/reduce_scatter | solution.py:217
  1011.3 5.4 multiply_reduce_fusion.2
  1018.6 4.6 all-reduce.5
  1023.2 74.9 %all-reduce.4 = (f32[3]{0:T(128)}, f32[4,768]{1,0:T(4,128)}, f32[8]{0:T(128)}, f32[8]{0:T(128)}) all-reduce(f32[3]{0:T(128)S(1)} %pad_maximum_fusion.9, f32[4,768]{1,0:T(4,128)} %get-tuple-element.94, f32[8]{0:T(128)} %get-tuple-element.95, f32[8]{0:T(128)} %get-tuple-element.96), channel_id=1, replica_groups=mesh['dp'=16,'mp'=2] {'dp'}, use_global_device_ids=true, to_apply=%region_21.22 | all-reduce | flops 3091 | bytes 24728 | tf_op jit(solution)/shard_map/psum | solution.py:150
  (276 shorter events, 94.0 us)
Async XLA Ops:
  7.2 69.2 %all-gather.6.cloned.1.call-start = ((), (), s32[]{:S(2)}) async-start(), calls=%async_computation.4 | async-start | bytes 2506752 | tf_op jit(solution)/shard_map/all_gather | solution.py:85
  9.0 214.2 %all-gather.4.cloned.1.call-start = ((), (), s32[]{:S(2)}) async-start(), calls=%async_computation.3 | async-start | bytes 12533760 | tf_op jit(solution)/shard_map/all_gather | solution.py:88
  11.4 247.6 %all-reduce.11.cloned.1.call-start = ((), (), s32[]{:S(2)}) async-start(), calls=%async_computation.5 | async-start | bytes 2359296 | tf_op jit(solution)/shard_map/psum | solution.py:134
  12.7 220.8 %copy-start.67 = (pred[384]{0:T(512)(128)(4,1)}, pred[384]{0:T(512)(128)(4,1)S(1)}, u32[]{:S(2)}) copy-start(pred[384]{0:T(512)(128)(4,1)S(1)} %broadcast_compare_fusion.1) | copy-start | bytes 1156
  84.1 149.4 %copy-start.23 = (bf16[384,768]{1,0:T(8,128)(2,1)S(1)}, bf16[384,768]{1,0:T(8,128)(2,1)}, u32[]{:S(2)}) copy-start(bf16[384,768]{1,0:T(8,128)(2,1)} %param.17) | copy-start | bytes 1769476
  84.1 149.4 %copy-start.26 = (bf16[3,768,384]{1,2,0:T(8,128)(2,1)S(1)}, bf16[3,768,384]{1,2,0:T(8,128)(2,1)}, u32[]{:S(2)}) copy-start(bf16[3,768,384]{1,2,0:T(8,128)(2,1)} %copy.136) | copy-start | bytes 5308420
  240.9 124.2 %all-gather.8.cloned.1.call-start = ((), (), s32[]{:S(2)}) async-start(), calls=%async_computation.6 | async-start | bytes 7520256 | tf_op jit(solution)/shard_map/all_gather | solution.py:86
  243.0 152.1 %all-reduce.13.cloned.1.call-start = ((), (), s32[]{:S(2)}) async-start(), calls=%async_computation.7 | async-start | bytes 2359296 | tf_op jit(solution)/shard_map/psum | solution.py:141
  261.1 134.0 %copy-start.47 = (f32[384]{0:T(512)}, f32[384]{0:T(512)S(1)}, u32[]{:S(2)}) copy-start(f32[384]{0:T(512)S(1)} %broadcast_multiply_fusion.5) | copy-start | bytes 4612
  377.0 55.5 %all-reduce.15.cloned.1.call-start = ((), (), s32[]{:S(2)}) async-start(), calls=%async_computation.8 | async-start | bytes 2359296 | tf_op jit(solution)/shard_map/psum | solution.py:162
  411.4 57.0 %all-reduce.17.cloned.1.call-start = ((), (), s32[]{:S(2)}) async-start(), calls=%async_computation.9 | async-start | bytes 1179648 | tf_op jit(solution)/shard_map/psum | solution.py:209
  448.2 563.0 %reduce-scatter.2.cloned.1.call-start = ((), (), s32[]{:S(2)}) async-start(), calls=%async_computation.10 | async-start | bytes 25067520 | tf_op jit(solution)/shard_map/reduce_scatter | solution.py:217
  492.9 89.7 %all-to-all-start = ((bf16[16,4,48,384]{3,2,1,0:T(8,128)(2,1)}), bf16[16,4,48,384]{3,2,1,0:T(8,128)(2,1)S(1)}, u32[]{:S(2)}, u32[]{:S(2)}) async-start(bf16[16,4,48,384]{3,2,1,0:T(8,128)(2,1)} %copy.121), calls=%async_computation | async-start | bytes 4718592 | tf_op jit(solution)/shard_map/all_to_all | solution.py:26
  516.2 320.1 %copy-start.66 = (f32[768]{0:T(1024)S(1)}, f32[768]{0:T(1024)}, u32[]{:S(2)}) copy-start(f32[768]{0:T(1024)} %get-tuple-element.73) | copy-start | bytes 9220
  516.2 320.1 %copy-start.65 = (f32[768]{0:T(1024)S(1)}, f32[768]{0:T(1024)}, u32[]{:S(2)}) copy-start(f32[768]{0:T(1024)} %get-tuple-element.80) | copy-start | bytes 9220
  516.2 322.1 %copy-start.63 = (f32[768]{0:T(1024)S(1)}, f32[768]{0:T(1024)}, u32[]{:S(2)}) copy-start(f32[768]{0:T(1024)} %get-tuple-element.71) | copy-start | bytes 9220
  516.2 322.1 %copy-start.62 = (f32[768]{0:T(1024)S(1)}, f32[768]{0:T(1024)}, u32[]{:S(2)}) copy-start(f32[768]{0:T(1024)} %get-tuple-element.77) | copy-start | bytes 9220
  582.6 258.4 %all-to-all-start.1 = ((bf16[16,3,48,1536]{3,2,1,0:T(8,128)(2,1)}), bf16[16,3,48,1536]{3,2,1,0:T(8,128)(2,1)}, u32[]{:S(2)}, u32[]{:S(2)}) async-start(bf16[16,3,48,1536]{3,2,1,0:T(8,128)(2,1)} %maximum_bitcast_fusion), calls=%async_computation.1 | async-start | bytes 14155776 | tf_op jit(solution)/shard_map/all_to_all | solution.py:26
  612.6 226.7 %copy-start.21 = (f32[4,48,384]{2,1,0:T(8,128)S(1)}, f32[4,48,384]{2,1,0:T(8,128)}, u32[]{:S(2)}) copy-start(f32[4,48,384]{2,1,0:T(8,128)} %param.22) | copy-start | bytes 884740
  612.6 226.7 %copy-start.42 = (f32[4,48,384]{2,1,0:T(8,128)S(1)}, f32[4,48,384]{2,1,0:T(8,128)}, u32[]{:S(2)}) copy-start(f32[4,48,384]{2,1,0:T(8,128)} %param.23) | copy-start | bytes 884740
  612.6 226.7 %copy-start.43 = (f32[4,48,384]{2,1,0:T(8,128)S(1)}, f32[4,48,384]{2,1,0:T(8,128)}, u32[]{:S(2)}) copy-start(f32[4,48,384]{2,1,0:T(8,128)} %param.24) | copy-start | bytes 884740
  845.7 165.5 %copy-start.3 = (f32[960,384]{1,0:T(8,128)S(1)}, f32[960,384]{1,0:T(8,128)}, u32[]{:S(2)}) copy-start(f32[960,384]{1,0:T(8,128)} %param.28) | copy-start | bytes 4423684
  848.2 258.0 %copy-start.19 = (f32[3,48,1536]{2,1,0:T(8,128)}, f32[3,48,1536]{2,1,0:T(8,128)S(1)}, u32[]{:S(2)}) copy-start(f32[3,48,1536]{2,1,0:T(8,128)S(1)} %get-tuple-element.105) | copy-start | bytes 2654212
  848.2 253.1 %copy-start.46 = (f32[4,768]{1,0:T(4,128)S(1)}, f32[4,768]{1,0:T(4,128)}, u32[]{:S(2)}) copy-start(f32[4,768]{1,0:T(4,128)} %param.31) | copy-start | bytes 36868
  (71 other events, 528.5 us)
Sparse Core Ops, SparseCore 0:
  11.4 64.9 all-gather.5
  79.8 143.3 all-gather.3
  241.1 17.9 all-reduce.10
  262.6 102.5 all-gather.7
  377.1 17.9 all-reduce.12
  411.5 20.9 all-reduce.14
  448.3 20.0 all-reduce.16
  483.5 527.7 reduce-scatter.1
